TPU v7x, 512 devices: a whole 4x4x16 slice. The times are simulated.
512 devices in a mesh: cells: 32 (over z, core), genes: 16 (over x, y).
Axes of the slice: x: 4, y: 4, z: 16, core: 2. Of those that a mesh axis runs over, the one named last changes fastest.
Arguments:
- sketch: bfloat16 [32768, 256], P('cells'), may hold values from -6 to 6
- tiles: bfloat16 [49152, 128, 128], P(('cells', 'genes')), may hold values from -0.0546875 to 0.0546875
- tile_rows: int32 [49152], P(('cells', 'genes')), may hold values from 0 to 7, as said below
- tile_cols: int32 [49152], P(('cells', 'genes')), may hold values from 0 to 15
- tile_counts: int32 [512], P(('cells', 'genes')), may hold values from 16 to 96, as said below
Outputs:
- projected: float32 [32768, 256], P(('cells', 'genes'))
Inputs may be any that keep to these rules, and one draw needn't show every extreme that they name: Within one device's slots the pairs (tile_rows, tile_cols) are distinct. `tile_counts`: some device holds 96 tiles and the device half the cells axis away from it holds 16.
All inputs are finite; a program needn't handle non-finite values.
Results may differ from a plain program's by a relative error of at most 0.0021.
Values may be sent and summed in bfloat16 or wider, within the bound.
A program may use at most 128 MiB of HBM per device.

v0:
```python
import jax
import jax.numpy as jnp
from jax import lax
from jax.sharding import PartitionSpec as P

GENE_BLOCKS = 16


def selector(index_ids, slot_live, width):
    hits = (index_ids[:, None] == jnp.arange(width, dtype=jnp.int32)[None, :]).astype(jnp.float32)
    return hits * slot_live[:, None]


def local(sketch, tiles, tile_rows, tile_cols, tile_counts):
    tile_size = tiles.shape[1]
    sketch_width = sketch.shape[1]
    slot_total = tiles.shape[0]
    row_blocks = sketch.shape[0] // tile_size
    sketch_blocks = sketch.reshape(row_blocks, tile_size, sketch_width)
    slot_live = (jnp.arange(slot_total, dtype=jnp.int32) < tile_counts[0]).astype(jnp.float32)
    col_select = selector(tile_cols, slot_live, GENE_BLOCKS)
    row_select = selector(tile_rows, slot_live, row_blocks)
    picked_rows = sketch_blocks[tile_rows]
    first_terms = jnp.einsum("ski,skr->sir", tiles, picked_rows, preferred_element_type=jnp.float32)
    gene_acc = jnp.einsum("sg,sir->gir", col_select, first_terms, precision=lax.Precision.HIGHEST)
    gene_cast = lax.psum(gene_acc, "cells").astype(jnp.bfloat16)
    picked_genes = gene_cast[tile_cols]
    second_terms = jnp.einsum(
        "sik,skr->sir", tiles, picked_genes, preferred_element_type=jnp.float32
    )
    cell_acc = jnp.einsum("sb,sir->bir", row_select, second_terms, precision=lax.Precision.HIGHEST)
    return lax.psum_scatter(
        cell_acc.reshape(row_blocks * tile_size, sketch_width),
        "genes",
        scatter_dimension=0,
        tiled=True,
    )


def solution(mesh):
    in_specs = (
        P("cells", None),
        P(("cells", "genes"), None, None),
        P(("cells", "genes")),
        P(("cells", "genes")),
        P(("cells", "genes")),
    )
    out_specs = P(("cells", "genes"), None)
    return jax.shard_map(local, mesh=mesh, in_specs=in_specs, out_specs=out_specs, check_vma=False)
```

profile of v0, /device:TPU:1, one launch (start us, length us, event | category | flops | bytes accessed | tf_op | source)
XLA Modules:
  0.0 301.1 jit_solution(11839636375966423922)
XLA Ops:
  6.5 0.0 copy-start
  6.5 0.0 reduce-scatter.2.cloned.1.call-start
  7.4 0.8 compare_select_fusion.1
  8.2 7.0 %gather_fusion = bf16[96,128,256]{2,1,0:T(8,128)(2,1)} fusion(bf16[8,128,256]{2,1,0:T(8,128)(2,1)} %bitcast.20, s32[1024]{0:T(1024)S(1)} %pad_clamp_fusion.1), kind=kCustom, calls=%fused_computation | custom fusion | bytes 12583296 | tf_op jit(solution)/shard_map/gather | solution.py:23
  15.1 0.0 copy-done
  15.1 9.2 %convolution_bitcast_fusion = f32[96,128,256]{1,2,0:T(8,128)} fusion(bf16[96,128,256]{2,1,0:T(8,128)(2,1)} %gather_fusion, bf16[96,128,128]{2,1,0:T(8,128)(2,1)S(1)} %copy-done), kind=kOutput, calls=%fused_computation.4 | convolution fusion | flops 805306368 | bytes 22020096 | tf_op jit(solution)/shard_map/ski,skr->sir/dot_general | solution.py:24
  24.3 0.0 copy-start.1
  24.3 12.7 %copy.7 = f32[96,128,256]{2,0,1:T(8,128)} copy(f32[96,128,256]{1,2,0:T(8,128)} %convolution_bitcast_fusion) | data formatting | bytes 25165824 | tf_op jit(solution)/shard_map/ski,skr->sir/dot_general | solution.py:24
  37.0 0.0 copy-done.1
  37.0 9.1 %fusion.2 = f32[16,128,256]{2,0,1:T(8,128)S(1)} fusion(f32[96,128,256]{2,0,1:T(8,128)} %copy.7, f32[96]{0:T(128)S(1)} %compare_convert_fusion, s32[96]{0:T(128)S(1)} %copy-done.1), kind=kOutput, calls=%fused_computation.5 | convolution fusion | flops 603982848 | bytes 14680832 | tf_op jit(solution)/shard_map/sg,sir->gir/dot_general | solution.py:25
  46.1 2.6 copy.8
  48.7 119.7 %all-reduce.1 = bf16[16,128,256]{2,1,0:T(8,128)(2,1)} all-reduce(f32[16,128,256]{2,1,0:T(8,128)} %copy.8), channel_id=1, replica_groups=mesh['cells'=32,'genes'=16] {'cells'}, use_global_device_ids=true, to_apply=%region_0.0 | all-reduce | flops 524288 | bytes 3145728 | tf_op jit(solution)/shard_map/psum | solution.py:26
  168.3 7.2 %gather_fusion.1 = bf16[96,128,256]{2,1,0:T(8,128)(2,1)} fusion(bf16[16,128,256]{2,1,0:T(8,128)(2,1)} %all-reduce.1, s32[1024]{0:T(1024)S(1)} %pad_clamp_fusion), kind=kCustom, calls=%fused_computation.1 | custom fusion | bytes 12583296 | tf_op jit(solution)/shard_map/gather | solution.py:27
  175.5 9.2 %fusion.15 = f32[96,256,128]{2,1,0:T(8,128)} fusion(bf16[96,128,256]{2,1,0:T(8,128)(2,1)} %gather_fusion.1, bf16[96,128,128]{2,1,0:T(8,128)(2,1)S(1)} %copy-done), kind=kOutput, calls=%fused_computation.25 | convolution fusion | flops 805306368 | bytes 22020096 | tf_op jit(solution)/shard_map/sik,skr->sir/dot_general | solution.py:28
  184.7 0.0 copy-start.2
  184.7 12.7 %copy.9 = f32[96,256,128]{1,0,2:T(8,128)} copy(f32[96,256,128]{2,1,0:T(8,128)} %fusion.15) | data formatting | bytes 25165824 | tf_op jit(solution)/shard_map/sik,skr->sir/dot_general | solution.py:28
  197.4 0.0 copy-done.2
  197.4 8.9 %fusion = f32[8,128,256]{2,0,1:T(8,128)S(1)} fusion(f32[96,256,128]{1,0,2:T(8,128)} %copy.9, f32[96]{0:T(128)S(1)} %compare_convert_fusion, s32[96]{0:T(128)S(1)} %copy-done.2), kind=kOutput, calls=%fused_computation.2 | convolution fusion | flops 301991424 | bytes 13632256 | tf_op jit(solution)/shard_map/sb,sir->bir/dot_general | solution.py:31
  206.3 1.3 copy.6
  207.6 0.0 reduce-scatter.2.cloned.1.call-update
  207.7 86.6 %reduce-scatter.2.cloned.1.call-done = f32[64,256]{1,0:T(8,128)} async-done(((f32[1024,256]{1,0:T(8,128)}), f32[64,256]{1,0:T(8,128)}) %reduce-scatter.2.cloned.1.call-update) | async-done | bytes 65552 | tf_op jit(solution)/shard_map/reduce_scatter | solution.py:32
  (4 shorter events, 0.0 us)
Async XLA Ops:
  6.5 8.6 %copy-start = (bf16[96,128,128]{2,1,0:T(8,128)(2,1)S(1)}, bf16[96,128,128]{2,1,0:T(8,128)(2,1)}, u32[]{:S(2)}) copy-start(bf16[96,128,128]{2,1,0:T(8,128)(2,1)} %param.6) | copy-start | bytes 9437188
  6.5 287.7 %reduce-scatter.2.cloned.1.call-start = ((), (), s32[]{:S(2)}) async-start(), calls=%async_computation.1 | async-start | bytes 1114112 | tf_op jit(solution)/shard_map/reduce_scatter | solution.py:32
  24.3 12.7 %copy-start.1 = (s32[96]{0:T(128)S(1)}, s32[96]{0:T(128)}, u32[]{:S(2)}) copy-start(s32[96]{0:T(128)} %param.8) | copy-start | bytes 1156
  184.7 12.7 %copy-start.2 = (s32[96]{0:T(128)S(1)}, s32[96]{0:T(128)}, u32[]{:S(2)}) copy-start(s32[96]{0:T(128)} %param.7) | copy-start | bytes 1156
Sparse Core Ops, SparseCore 0:
  207.8 86.4 reduce-scatter.1
where the time goes:
time: 302 us; the launch traced here: 301 us
  blocking collectives  120 us (40%)
  waiting for transfers between devices  86.6 us (29%)
  local copies, waits for them, and re-layouts  43.4 us (14%)
  matrix products  36.3 us (12%)
  between operations  14.2 us (5%)
    psum x1, blocking collectives, local(): gene_cast = lax.psum(gene_acc, 'cells').astype(jnp.bfloat16)  120 us
    reduce_scatter x1, waiting for transfers between devices, local(): lax.psum_scatter(cell_acc.reshape(row_blocks * tile_size, sketch_width),...  86.6 us
    dot_general x1, local copies, waits for them, and re-layouts, local(): jnp.einsum('sik,skr->sir', tiles, picked_genes, preferred_element_type=jn...  12.7 us
    dot_general x1, local copies, waits for them, and re-layouts, local(): jnp.einsum('ski,skr->sir', tiles, picked_rows, preferred_element_type=jnp...  12.7 us
    dot_general x1, matrix products, local(): jnp.einsum('ski,skr->sir', tiles, picked_rows, preferred_element_type=jnp...  9.19 us
    dot_general x1, matrix products, local(): jnp.einsum('sik,skr->sir', tiles, picked_genes, preferred_element_type=jn...  9.19 us
    dot_general x1, matrix products, local(): jnp.einsum('sg,sir->gir', col_select, first_terms, precision=lax.Precisio...  9.05 us
    dot_general x1, matrix products, local(): jnp.einsum('sb,sir->bir', row_select, second_terms, precision=lax.Precisi...  8.9 us
  transfers between devices with their start and end apart: 1, of which 1 were waited for; matrix products, arithmetic and copies ran while one was open for 0% of the time, Pallas kernels for 0%

commit v1 on v0

v1 whole, which is shorter than its diff:
```python
import functools

import jax
import jax.numpy as jnp
from jax import lax
from jax.experimental import pallas as pl
from jax.experimental.pallas import tpu as pltpu
from jax.sharding import PartitionSpec as P

MESH = pl.DeviceIdType.MESH
TILE = 128
RS_PIECES = 4
AG_PIECES = 2
F32 = jnp.float32
BF16 = jnp.bfloat16


def mult(value, of):
    return pl.multiple_of(value, of)


def kernel(
    nz, side, sketch_hbm, tiles_hbm, rows_hbm, cols_hbm, count_hbm, out_ref,
    tiles, sketch, ids_r, ids_c, count, slot_v, slot_s, dense, qt, own, oth, prt,
    first, rr, gath, ysend, yown, yrecv,
    in_sem, prt_send, prt_recv, rs_send, rs_recv, ag_send, ag_recv, pg_send, pg_recv, y_send, y_recv,
):
    slots = tiles_hbm.shape[0]
    rank = sketch_hbm.shape[1]
    nh = nz // 2
    half = nz // 2 * TILE
    blocks = nz
    row_blocks = sketch_hbm.shape[0] // TILE
    pr = TILE // RS_PIECES
    pa = TILE // AG_PIECES

    cells = lax.axis_index("cells")
    genes = lax.axis_index("genes")
    z, core = cells // 2, cells % 2
    gx, gy = genes // side, genes % side
    right = ((z + 1) % nz * 2 + core, genes)
    left = ((z + nz - 1) % nz * 2 + core, genes)
    twin = (z * 2 + 1 - core, genes)
    ring = (right, left)

    def peer(ox, oy):
        return (cells, (gx + ox) % side * side + (gy + oy) % side)

    offsets = [(ox, oy) for ox in range(side) for oy in range(side)][1:]

    loads = [
        pltpu.make_async_copy(rows_hbm, ids_r, in_sem.at[0]),
        pltpu.make_async_copy(cols_hbm, ids_c, in_sem.at[1]),
        pltpu.make_async_copy(count_hbm, count, in_sem.at[2]),
        pltpu.make_async_copy(sketch_hbm, sketch, in_sem.at[3]),
        pltpu.make_async_copy(tiles_hbm, tiles.at[pl.ds(0, slots)], in_sem.at[4]),
    ]
    for load in loads:
        load.start()

    barrier = pltpu.get_barrier_semaphore()
    greeted = [right, left, twin] + [peer(ox, oy) for ox, oy in offsets]
    for who in greeted:
        pl.semaphore_signal(barrier, inc=1, device_id=who, device_id_type=MESH)

    tiles[slots] = jnp.zeros((TILE, TILE), BF16)
    for load in loads[:3]:
        load.wait()
    lane = lax.broadcasted_iota(jnp.int32, (1, slots), 1)
    key = jnp.where(lane < count[0], ids_r[...] * blocks + ids_c[...], -1)
    total = row_blocks * blocks
    where_j = lax.broadcasted_iota(jnp.int32, (total, slots), 0)
    which_s = lax.broadcasted_iota(jnp.int32, (total, slots), 1)
    hit = where_j == jnp.broadcast_to(key, (total, slots))
    picked = jnp.sum(jnp.where(hit, which_s - slots, 0), axis=1, keepdims=True) + slots
    diag = lax.broadcasted_iota(jnp.int32, (total, total), 0) == lax.broadcasted_iota(jnp.int32, (total, total), 1)
    row = jnp.sum(jnp.where(diag, jnp.broadcast_to(picked, (total, total)), 0), axis=0, keepdims=True)
    slot_v[...] = row
    to_smem = pltpu.make_async_copy(slot_v, slot_s, in_sem.at[5])
    to_smem.start()

    loads[3].wait()
    qt[...] = jnp.transpose(sketch[...])
    to_smem.wait()
    loads[4].wait()

    def place(r, carry):
        at = mult(r * TILE, TILE)
        for c in range(blocks):
            dense[pl.ds(at, TILE), c * TILE:(c + 1) * TILE] = tiles[jnp.clip(slot_s[0, r * blocks + c], 0, slots)]
        return carry
    lax.fori_loop(0, row_blocks, place, 0)

    pl.semaphore_wait(barrier, len(greeted))

    def product(offset, into):
        value = jnp.dot(qt[...], dense[:, pl.ds(mult(offset, 2 * TILE), 2 * TILE)], preferred_element_type=F32)
        into[0] = value[:, :TILE]
        into[1] = value[:, TILE:]

    pending = []
    swaps = []
    for q in range(nh // 2):
        product((1 - core) * half + q * 2 * TILE, oth.at[pl.ds(2 * q, 2)])
        swap = pltpu.make_async_remote_copy(
            oth.at[pl.ds(2 * q, 2)], prt.at[pl.ds(2 * q, 2)], prt_send.at[q], prt_recv.at[q],
            device_id=twin, device_id_type=MESH)
        swap.start()
        swaps.append(swap)
        pending.append(swap)
    for q in range(nh // 2):
        product(core * half + q * 2 * TILE, own.at[pl.ds(2 * q, 2)])
    for swap in swaps:
        swap.wait_recv()

    def mine(d, p):
        at = mult(d % 2 * TILE + p * pr, pr)
        return own[d // 2, pl.ds(at, pr), :] + prt[d // 2, pl.ds(at, pr), :]

    def hops(way, p):
        return nh - (way + p) % 2

    def toward(way, n):
        return (z + n) % nz if way == 0 else (z + nz - n) % nz

    def rs_copy(way, step, p, source):
        return pltpu.make_async_remote_copy(
            source, rr.at[way, step, pl.ds(p * pr, pr)], rs_send.at[way, step, p], rs_recv.at[way, step, p],
            device_id=ring[way], device_id_type=MESH)

    for p in range(RS_PIECES):
        for way in range(2):
            first[way, pl.ds(p * pr, pr)] = mine(toward(way, hops(way, p)), p)
            copy = rs_copy(way, 0, p, first.at[way, pl.ds(p * pr, pr)])
            copy.start()
            pending.append(copy)
    for s in range(1, nh + 1):
        for p in range(RS_PIECES):
            for way in range(2):
                n = hops(way, p)
                if s > n:
                    continue
                landed = rr.at[way, s - 1, pl.ds(p * pr, pr)]
                rs_copy(way, s - 1, p, landed).wait_recv()
                if s < n:
                    landed[...] = landed[...] + mine(toward(way, n - s), p)
                    copy = rs_copy(way, s, p, landed)
                    copy.start()
                    pending.append(copy)
    done = []
    for p in range(RS_PIECES):
        rows = pl.ds(p * pr, pr)
        done.append(mine(z, p) + rr[0, hops(0, p) - 1, rows] + rr[1, hops(1, p) - 1, rows])
    reduced = jnp.transpose(jnp.concatenate(done, axis=0)).astype(BF16)

    def place_of(who, d, p):
        return gath.at[pl.ds(mult(who * half + d // 2 * TILE + p * pa, pa), pa), pl.ds(mult(d % 2 * TILE, TILE), TILE)]

    def ag_copy(way, step, p, d):
        there = place_of(core, d, p)
        return pltpu.make_async_remote_copy(
            there, there, ag_send.at[way, step, p], ag_recv.at[way, step, p], device_id=ring[way], device_id_type=MESH)

    def pg_copy(index, p, who, d):
        there = place_of(who, d, p)
        return pltpu.make_async_remote_copy(
            there, there, pg_send.at[index, p], pg_recv.at[index, p], device_id=twin, device_id_type=MESH)

    arrivals = []
    for p in range(AG_PIECES):
        place_of(core, z, p)[...] = reduced[p * pa:(p + 1) * pa]
        for copy in [ag_copy(way, 0, p, z) for way in range(2)] + [pg_copy(0, p, core, z)]:
            copy.start()
            pending.append(copy)
        arrivals.append((0, p, z))
    for s in range(1, nh + 1):
        for p in range(AG_PIECES):
            for way in range(2):
                n = hops(way, p)
                if s > n:
                    continue
                d = toward(1 - way, s)
                ag_copy(way, s - 1, p, d).wait_recv()
                index = 1 + way * nh + s - 1
                onward = [pg_copy(index, p, core, d)]
                if s < n:
                    onward.insert(0, ag_copy(way, s, p, d))
                for copy in onward:
                    copy.start()
                    pending.append(copy)
                arrivals.append((index, p, d))
    for index, p, d in arrivals:
        pg_copy(index, p, 1 - core, d).wait_recv()

    keep = side * side
    part = dense.shape[0] // keep
    wide = part * side
    landings = []
    order = [side // 2] + [o for o in range(1, side) if o != side // 2] + [0]
    for ox in order:
        at = mult((gx + ox) % side * wide, wide)
        value = jnp.dot(dense[pl.ds(at, wide), :], gath[...], preferred_element_type=F32)
        if ox == 0:
            yown[...] = value
        ysend[ox] = value.astype(BF16)
        for oy in order:
            if ox == 0 and oy == 0:
                continue
            index = ox * side + oy
            copy = pltpu.make_async_remote_copy(
                ysend.at[ox, pl.ds(mult((gy + oy) % side * part, part), part)], yrecv.at[index],
                y_send.at[index], y_recv.at[index], device_id=peer(ox, oy), device_id_type=MESH)
            copy.start()
            pending.append(copy)
            landings.append((index, copy))
    result = yown[pl.ds(mult(gy * part, part), part), :]
    for index, copy in landings:
        copy.wait_recv()
        result = result + yrecv[index].astype(F32)
    out_ref[...] = result
    for copy in pending:
        copy.wait_send()


def solution(mesh):
    nz = mesh.shape["cells"] // 2
    side = {16: 4, 4: 2}[mesh.shape["genes"]]
    nh = nz // 2

    def local(sketch, tiles, tile_rows, tile_cols, tile_counts):
        slots = tiles.shape[0]
        rows, rank = sketch.shape
        part = rows // (side * side)
        dma = pltpu.SemaphoreType.DMA
        hbm = pl.BlockSpec(memory_space=pl.ANY)
        vmem = pltpu.VMEM
        return pl.pallas_call(
            functools.partial(kernel, nz, side),
            out_shape=jax.ShapeDtypeStruct((part, rank), F32),
            in_specs=[hbm] * 5,
            out_specs=pl.BlockSpec(memory_space=pltpu.VMEM),
            scratch_shapes=[
                vmem((slots + 1, TILE, TILE), BF16),
                vmem((rows, rank), BF16),
                vmem((1, slots), jnp.int32),
                vmem((1, slots), jnp.int32),
                pltpu.SMEM((1,), jnp.int32),
                vmem((1, rows // TILE * nz), jnp.int32),
                pltpu.SMEM((1, rows // TILE * nz), jnp.int32),
                vmem((rows, nz * TILE), BF16),
                vmem((rank, rows), BF16),
                vmem((nh, rank, TILE), F32),
                vmem((nh, rank, TILE), F32),
                vmem((nh, rank, TILE), F32),
                vmem((2, TILE, TILE), F32),
                vmem((2, nh, TILE, TILE), F32),
                vmem((nz * TILE, rank), BF16),
                vmem((side, part * side, rank), BF16),
                vmem((part * side, rank), F32),
                vmem((side * side, part, rank), BF16),
                dma((6,)),
                dma((nh // 2,)),
                dma((nh // 2,)),
                dma((2, nh, RS_PIECES)),
                dma((2, nh, RS_PIECES)),
                dma((2, nh, AG_PIECES)),
                dma((2, nh, AG_PIECES)),
                dma((1 + 2 * nh, AG_PIECES)),
                dma((1 + 2 * nh, AG_PIECES)),
                dma((side * side,)),
                dma((side * side,)),
            ],
            compiler_params=pltpu.CompilerParams(
                collective_id=0, has_side_effects=True, vmem_limit_bytes=67_000_000),
            name="power_pass",
        )(sketch, tiles, tile_rows.reshape(1, -1), tile_cols.reshape(1, -1), tile_counts)

    in_specs = (
        P("cells", None),
        P(("cells", "genes"), None, None),
        P(("cells", "genes")),
        P(("cells", "genes")),
        P(("cells", "genes")),
    )
    return jax.shard_map(
        local, mesh=mesh, in_specs=in_specs, out_specs=P(("cells", "genes"), None), check_vma=False)
```

time: 302 us -> 85.9 us (0.28)
  blocking collectives: 120 us -> 0 us
  waiting for transfers between devices: 86.6 us -> 0 us
  Pallas kernels: 0 us -> 83.5 us
  local copies, waits for them, and re-layouts: 43.4 us -> 1.47 us
  matrix products: 36.3 us -> 0 us
  between operations: 14.2 us -> 0.66 us
    psum x1 -> x0, blocking collectives: 120 us -> none  [local(): gene_cast = lax.psum(gene_acc, 'cells').astype(jnp.bfloat16)]
    reduce_scatter x1 -> x0, waiting for transfers between devices: 86.6 us -> none  [local(): lax.psum_scatter(cell_acc.reshape(row_blocks * tile_size, sketch_width),...]
    pallas_call x0 -> x1, Pallas kernels: none -> 83.5 us  [local(): pl.pallas_call(functools.partial(kernel, nz, side), out_shape=jax.ShapeDt...]
    dot_general x4 -> x0, matrix products: 36.3 us -> none  [the longest x1 9.19 us: local(): jnp.einsum('ski,skr->sir', tiles, picked_rows, preferred_element_type=jnp...]
    dot_general x4 -> x0, local copies, waits for them, and re-layouts: 29.3 us -> none  [the longest x1 12.7 us: local(): jnp.einsum('sik,skr->sir', tiles, picked_genes, preferred_element_type=jn...]
    gather x2 -> x0, local copies, waits for them, and re-layouts: 14.1 us -> none  [the longest x1 7.17 us: local(): picked_genes = gene_cast[tile_cols]]
  transfers between devices with their start and end apart: 1 -> 0, of which waited for: 1 -> 0; matrix products, arithmetic and copies ran while one was open for 0% -> 0% of each run, Pallas kernels for 0% -> 0%
where the time goes in v1:
time: 85.9 us; the launch traced here: 85.7 us
  Pallas kernels  83.5 us (97%)
  local copies, waits for them, and re-layouts  1.47 us (2%)
    pallas_call x1, Pallas kernels, local(): pl.pallas_call(functools.partial(kernel, nz, side), out_shape=jax.ShapeDt...  83.5 us

profile of v1, /device:TPU:1, one launch (start us, length us, event | category | flops | bytes accessed | tf_op | source)
XLA Modules:
  0.0 85.7 jit_solution(12608106020788517004)
XLA Ops:
  0.7 83.5 %power_pass.1 = f32[64,256]{1,0:T(8,128)} custom-call(bf16[1024,256]{1,0:T(8,128)(2,1)} %sketch_hbm.1, bf16[96,128,128]{2,1,0:T(8,128)(2,1)} %tiles_hbm.1, s32[1,96]{1,0:T(1,128)} %bitcast.2, s32[1,96]{1,0:T(1,128)} %bitcast.3, s32[1]{0:T(128)S(6)} %copy.7.count_hbm), custom_call_target="tpu_custom_call" | custom-call | tf_op jit(solution)/shard_map/power_pass/pallas_call | solution.py:237
  84.2 1.5 %copy.8 = f32[64,256]{1,0:T(8,128)} copy(f32[64,256]{1,0:T(8,128)} %power_pass.1) | data formatting | bytes 131072

commit v2 on v1

--- a/solution.py
+++ b/solution.py
@@ -9,8 +9,12 @@
 
 MESH = pl.DeviceIdType.MESH
 TILE = 128
-RS_PIECES = 4
-AG_PIECES = 2
+PIECES = 2
+CODED = True
+PEAK = 32700.0
+SCALE_ROWS = 16
+ORDER = (2, 1, 3, 0)
+UP = {1: 0, 2: 0, 3: 2, 4: 2, 5: 0, 6: 5, 7: 5, 8: 5}
 F32 = jnp.float32
 BF16 = jnp.bfloat16
 
@@ -31,22 +35,32 @@
     half = nz // 2 * TILE
     blocks = nz
     row_blocks = sketch_hbm.shape[0] // TILE
-    pr = TILE // RS_PIECES
-    pa = TILE // AG_PIECES
+    pr = TILE // PIECES
 
     cells = lax.axis_index("cells")
     genes = lax.axis_index("genes")
     z, core = cells // 2, cells % 2
     gx, gy = genes // side, genes % side
-    right = ((z + 1) % nz * 2 + core, genes)
-    left = ((z + nz - 1) % nz * 2 + core, genes)
     twin = (z * 2 + 1 - core, genes)
-    ring = (right, left)
+
+    def along(way, n):
+        return ((z + n) % nz if way == 0 else (z + nz - n) % nz)
+
+    def ring(way, n):
+        return (along(way, n) * 2 + core, genes)
+
+    steps = sorted({j - UP[j] for j in range(1, nh + 1)})
+    reach = sorted({n % nz for d in steps for n in (d, nz - d)})
 
     def peer(ox, oy):
         return (cells, (gx + ox) % side * side + (gy + oy) % side)
 
     offsets = [(ox, oy) for ox in range(side) for oy in range(side)][1:]
+
+    barrier = pltpu.get_barrier_semaphore()
+    greeted = [ring(0, n) for n in reach] + [twin] + [peer(ox, oy) for ox, oy in offsets]
+    for who in greeted:
+        pl.semaphore_signal(barrier, inc=1, device_id=who, device_id_type=MESH)
 
     loads = [
         pltpu.make_async_copy(rows_hbm, ids_r, in_sem.at[0]),
@@ -57,11 +71,6 @@
     ]
     for load in loads:
         load.start()
-
-    barrier = pltpu.get_barrier_semaphore()
-    greeted = [right, left, twin] + [peer(ox, oy) for ox, oy in offsets]
-    for who in greeted:
-        pl.semaphore_signal(barrier, inc=1, device_id=who, device_id_type=MESH)
 
     tiles[slots] = jnp.zeros((TILE, TILE), BF16)
     for load in loads[:3]:
@@ -91,25 +100,29 @@
         return carry
     lax.fori_loop(0, row_blocks, place, 0)
 
-    pl.semaphore_wait(barrier, len(greeted))
+    pairs = nh // 2
+    order_q = [(z // 4 + o) % pairs for o in ORDER if o < pairs]
 
     def product(offset, into):
         value = jnp.dot(qt[...], dense[:, pl.ds(mult(offset, 2 * TILE), 2 * TILE)], preferred_element_type=F32)
         into[0] = value[:, :TILE]
         into[1] = value[:, TILE:]
 
+    for q in order_q:
+        product((1 - core) * half + q * 2 * TILE, oth.at[pl.ds(2 * q, 2)])
+    for q in order_q:
+        product(core * half + q * 2 * TILE, own.at[pl.ds(2 * q, 2)])
+
+    pl.semaphore_wait(barrier, len(greeted))
     pending = []
     swaps = []
-    for q in range(nh // 2):
-        product((1 - core) * half + q * 2 * TILE, oth.at[pl.ds(2 * q, 2)])
+    for k, q in enumerate(order_q):
         swap = pltpu.make_async_remote_copy(
-            oth.at[pl.ds(2 * q, 2)], prt.at[pl.ds(2 * q, 2)], prt_send.at[q], prt_recv.at[q],
+            oth.at[pl.ds(2 * q, 2)], prt.at[pl.ds(2 * q, 2)], prt_send.at[k], prt_recv.at[k],
             device_id=twin, device_id_type=MESH)
         swap.start()
         swaps.append(swap)
         pending.append(swap)
-    for q in range(nh // 2):
-        product(core * half + q * 2 * TILE, own.at[pl.ds(2 * q, 2)])
     for swap in swaps:
         swap.wait_recv()
 
@@ -120,75 +133,98 @@
     def hops(way, p):
         return nh - (way + p) % 2
 
-    def toward(way, n):
-        return (z + n) % nz if way == 0 else (z + nz - n) % nz
-
-    def rs_copy(way, step, p, source):
+    def children(j, n):
+        return [c for c in range(1, n + 1) if UP[c] == j]
+
+    def encode(value, into):
+        if not CODED:
+            into[...] = value
+            return
+        peak = jnp.max(jnp.abs(value), axis=0, keepdims=True)
+        power = jnp.floor(jnp.log2(jnp.maximum(peak, 1e-30))) + 1.0
+        into[pl.ds(0, pr)] = jnp.round(value * (jnp.exp2(-power) * PEAK)).astype(jnp.int32).astype(jnp.int16)
+        into[pl.ds(pr, SCALE_ROWS)] = jnp.broadcast_to(power, (SCALE_ROWS, TILE)).astype(jnp.int32).astype(jnp.int16)
+
+    def decode(ref):
+        if not CODED:
+            return ref[...]
+        power = ref[pl.ds(pr, SCALE_ROWS)].astype(jnp.int32).astype(F32)[0:1]
+        return ref[pl.ds(0, pr)].astype(jnp.int32).astype(F32) * (jnp.exp2(power) * (1.0 / PEAK))
+
+    def rs_copy(way, j, p):
         return pltpu.make_async_remote_copy(
-            source, rr.at[way, step, pl.ds(p * pr, pr)], rs_send.at[way, step, p], rs_recv.at[way, step, p],
-            device_id=ring[way], device_id_type=MESH)
-
-    for p in range(RS_PIECES):
+            first.at[way, p, j - 1], rr.at[way, p, j - 1], rs_send.at[way, p, j - 1], rs_recv.at[way, p, j - 1],
+            device_id=ring(way, j - UP[j]), device_id_type=MESH)
+
+    def collect(way, j, p, total):
+        for c in children(j, hops(way, p)):
+            rs_copy(way, c, p).wait_recv()
+            total = total + decode(rr.at[way, p, c - 1])
+        return total
+
+    deep = [j for j in range(nh, 0, -1) if UP[j]]
+    heads = [j for j in range(nh, 0, -1) if not UP[j] and children(j, nh)]
+    near = [j for j in range(nh, 0, -1) if not UP[j] and not children(j, nh)]
+    for j in deep + heads + near:
+        for p in range(PIECES):
+            for way in range(2):
+                if j > hops(way, p):
+                    continue
+                encode(collect(way, j, p, mine(along(way, j), p)), first.at[way, p, j - 1])
+                copy = rs_copy(way, j, p)
+                copy.start()
+                pending.append(copy)
+    done = []
+    for p in range(PIECES):
+        total = mine(z, p)
         for way in range(2):
-            first[way, pl.ds(p * pr, pr)] = mine(toward(way, hops(way, p)), p)
-            copy = rs_copy(way, 0, p, first.at[way, pl.ds(p * pr, pr)])
-            copy.start()
-            pending.append(copy)
-    for s in range(1, nh + 1):
-        for p in range(RS_PIECES):
-            for way in range(2):
-                n = hops(way, p)
-                if s > n:
-                    continue
-                landed = rr.at[way, s - 1, pl.ds(p * pr, pr)]
-                rs_copy(way, s - 1, p, landed).wait_recv()
-                if s < n:
-                    landed[...] = landed[...] + mine(toward(way, n - s), p)
-                    copy = rs_copy(way, s, p, landed)
-                    copy.start()
-                    pending.append(copy)
-    done = []
-    for p in range(RS_PIECES):
-        rows = pl.ds(p * pr, pr)
-        done.append(mine(z, p) + rr[0, hops(0, p) - 1, rows] + rr[1, hops(1, p) - 1, rows])
+            total = collect(way, 0, p, total)
+        done.append(total)
     reduced = jnp.transpose(jnp.concatenate(done, axis=0)).astype(BF16)
 
     def place_of(who, d, p):
-        return gath.at[pl.ds(mult(who * half + d // 2 * TILE + p * pa, pa), pa), pl.ds(mult(d % 2 * TILE, TILE), TILE)]
-
-    def ag_copy(way, step, p, d):
+        return gath.at[pl.ds(mult(who * half + d // 2 * TILE + p * pr, pr), pr), pl.ds(mult(d % 2 * TILE, TILE), TILE)]
+
+    def ag_copy(way, j, p, d):
         there = place_of(core, d, p)
         return pltpu.make_async_remote_copy(
-            there, there, ag_send.at[way, step, p], ag_recv.at[way, step, p], device_id=ring[way], device_id_type=MESH)
+            there, there, ag_send.at[way, p, j - 1], ag_recv.at[way, p, j - 1],
+            device_id=ring(way, j - UP[j]), device_id_type=MESH)
 
     def pg_copy(index, p, who, d):
         there = place_of(who, d, p)
         return pltpu.make_async_remote_copy(
             there, there, pg_send.at[index, p], pg_recv.at[index, p], device_id=twin, device_id_type=MESH)
 
-    arrivals = []
-    for p in range(AG_PIECES):
-        place_of(core, z, p)[...] = reduced[p * pa:(p + 1) * pa]
-        for copy in [ag_copy(way, 0, p, z) for way in range(2)] + [pg_copy(0, p, core, z)]:
+    def spread(way, j, p, d):
+        for c in reversed(children(j, hops(way, p))):
+            copy = ag_copy(way, c, p, d)
             copy.start()
             pending.append(copy)
-        arrivals.append((0, p, z))
-    for s in range(1, nh + 1):
-        for p in range(AG_PIECES):
+
+    arrivals = []
+
+    def share(index, p, d):
+        copy = pg_copy(index, p, core, d)
+        copy.start()
+        pending.append(copy)
+        arrivals.append((index, p, d))
+
+    for p in range(PIECES):
+        place_of(core, z, p)[...] = reduced[p * pr:(p + 1) * pr]
+        for way in range(2):
+            spread(way, 0, p, z)
+    for p in range(PIECES):
+        share(0, p, z)
+    for j in heads[::-1] + near + deep[::-1]:
+        for p in range(PIECES):
             for way in range(2):
-                n = hops(way, p)
-                if s > n:
+                if j > hops(way, p):
                     continue
-                d = toward(1 - way, s)
-                ag_copy(way, s - 1, p, d).wait_recv()
-                index = 1 + way * nh + s - 1
-                onward = [pg_copy(index, p, core, d)]
-                if s < n:
-                    onward.insert(0, ag_copy(way, s, p, d))
-                for copy in onward:
-                    copy.start()
-                    pending.append(copy)
-                arrivals.append((index, p, d))
+                d = along(1 - way, j)
+                ag_copy(way, j, p, d).wait_recv()
+                spread(way, j, p, d)
+                share(1 + way * nh + j - 1, p, d)
     for index, p, d in arrivals:
         pg_copy(index, p, 1 - core, d).wait_recv()
 
@@ -232,6 +268,8 @@
         rows, rank = sketch.shape
         part = rows // (side * side)
         dma = pltpu.SemaphoreType.DMA
+        kind = jnp.int16 if CODED else F32
+        message = (2, PIECES, nh, TILE // PIECES + (SCALE_ROWS if CODED else 0), TILE)
         hbm = pl.BlockSpec(memory_space=pl.ANY)
         vmem = pltpu.VMEM
         return pl.pallas_call(
@@ -252,8 +290,8 @@
                 vmem((nh, rank, TILE), F32),
                 vmem((nh, rank, TILE), F32),
                 vmem((nh, rank, TILE), F32),
-                vmem((2, TILE, TILE), F32),
-                vmem((2, nh, TILE, TILE), F32),
+                vmem(message, kind),
+                vmem(message, kind),
                 vmem((nz * TILE, rank), BF16),
                 vmem((side, part * side, rank), BF16),
                 vmem((part * side, rank), F32),
@@ -261,12 +299,12 @@
                 dma((6,)),
                 dma((nh // 2,)),
                 dma((nh // 2,)),
-                dma((2, nh, RS_PIECES)),
-                dma((2, nh, RS_PIECES)),
-                dma((2, nh, AG_PIECES)),
-                dma((2, nh, AG_PIECES)),
-                dma((1 + 2 * nh, AG_PIECES)),
-                dma((1 + 2 * nh, AG_PIECES)),
+                dma((2, PIECES, nh)),
+                dma((2, PIECES, nh)),
+                dma((2, PIECES, nh)),
+                dma((2, PIECES, nh)),
+                dma((1 + 2 * nh, PIECES)),
+                dma((1 + 2 * nh, PIECES)),
                 dma((side * side,)),
                 dma((side * side,)),
             ],

time: 85.9 us -> 65.7 us (0.76)
  Pallas kernels: 83.5 us -> 63.4 us
    pallas_call x1, Pallas kernels: 83.5 us -> 63.4 us  [local(): pl.pallas_call(functools.partial(kernel, nz, side), out_shape=jax.ShapeDt...]
where the time goes in v2:
time: 65.7 us; the launch traced here: 65.5 us
  Pallas kernels  63.4 us (96%)
  local copies, waits for them, and re-layouts  1.47 us (2%)
  between operations  0.66 us (1%)
    pallas_call x1, Pallas kernels, local(): pl.pallas_call(functools.partial(kernel, nz, side), out_shape=jax.ShapeDt...  63.4 us
    unnamed x1, local copies, waits for them, and re-layouts  1.47 us

profile of v2, /device:TPU:1, one launch (start us, length us, event | category | flops | bytes accessed | tf_op | source)
XLA Modules:
  0.0 65.5 jit_solution(3928713715200876661)
XLA Ops:
  0.7 63.4 %power_pass.1 = f32[64,256]{1,0:T(8,128)} custom-call(bf16[1024,256]{1,0:T(8,128)(2,1)} %sketch_hbm.1, bf16[96,128,128]{2,1,0:T(8,128)(2,1)} %tiles_hbm.1, s32[1,96]{1,0:T(1,128)} %bitcast.2, s32[1,96]{1,0:T(1,128)} %bitcast.3, s32[1]{0:T(128)S(6)} %copy.7.count_hbm), custom_call_target="tpu_custom_call" | custom-call | tf_op jit(solution)/shard_map/power_pass/pallas_call | solution.py:275
  64.1 1.5 %copy.8 = f32[64,256]{1,0:T(8,128)} copy(f32[64,256]{1,0:T(8,128)} %power_pass.1) | data formatting | bytes 131072

commit v3 on v2

--- a/solution.py
+++ b/solution.py
@@ -27,7 +27,7 @@
     nz, side, sketch_hbm, tiles_hbm, rows_hbm, cols_hbm, count_hbm, out_ref,
     tiles, sketch, ids_r, ids_c, count, slot_v, slot_s, dense, qt, own, oth, prt,
     first, rr, gath, ysend, yown, yrecv,
-    in_sem, prt_send, prt_recv, rs_send, rs_recv, ag_send, ag_recv, pg_send, pg_recv, y_send, y_recv,
+    in_sem, prt_send, prt_recv, rs_send, rs_recv, ag_send, ag_recv, pg_send, pg_recv, y_send, y_recv, hint,
 ):
     slots = tiles_hbm.shape[0]
     rank = sketch_hbm.shape[1]
@@ -49,16 +49,18 @@
     def ring(way, n):
         return (along(way, n) * 2 + core, genes)
 
-    steps = sorted({j - UP[j] for j in range(1, nh + 1)})
+    steps = sorted({j - UP[j] for j in range(1, nh + 1)} & {1, 2, 3})
     reach = sorted({n % nz for d in steps for n in (d, nz - d)})
 
     def peer(ox, oy):
         return (cells, (gx + ox) % side * side + (gy + oy) % side)
 
     offsets = [(ox, oy) for ox in range(side) for oy in range(side)][1:]
+    close = [(ox, oy) for ox, oy in offsets if min(ox, side - ox) + min(oy, side - oy) <= 2]
+    hints = [(1, 0), (side - 1, 0), (1, 1)] if len(close) < len(offsets) else []
 
     barrier = pltpu.get_barrier_semaphore()
-    greeted = [ring(0, n) for n in reach] + [twin] + [peer(ox, oy) for ox, oy in offsets]
+    greeted = [ring(0, n) for n in reach] + [twin] + [peer(ox, oy) for ox, oy in close]
     for who in greeted:
         pl.semaphore_signal(barrier, inc=1, device_id=who, device_id_type=MESH)
 
@@ -114,6 +116,8 @@
         product(core * half + q * 2 * TILE, own.at[pl.ds(2 * q, 2)])
 
     pl.semaphore_wait(barrier, len(greeted))
+    for k, (ox, oy) in enumerate(hints):
+        pl.semaphore_signal(hint.at[k], inc=1, device_id=peer(side - ox, side - oy), device_id_type=MESH)
     pending = []
     swaps = []
     for k, q in enumerate(order_q):
@@ -123,11 +127,8 @@
         swap.start()
         swaps.append(swap)
         pending.append(swap)
-    for swap in swaps:
-        swap.wait_recv()
-
     def mine(d, p):
-        at = mult(d % 2 * TILE + p * pr, pr)
+        at = mult(p * TILE + d % 2 * pr, pr)
         return own[d // 2, pl.ds(at, pr), :] + prt[d // 2, pl.ds(at, pr), :]
 
     def hops(way, p):
@@ -165,25 +166,21 @@
     deep = [j for j in range(nh, 0, -1) if UP[j]]
     heads = [j for j in range(nh, 0, -1) if not UP[j] and children(j, nh)]
     near = [j for j in range(nh, 0, -1) if not UP[j] and not children(j, nh)]
+    ready = {deep[0]: swaps[:1], deep[1]: swaps[1:3], deep[-1]: swaps[3:]} if len(swaps) == 4 else {nh: swaps}
     for j in deep + heads + near:
+        for swap in ready.get(j, ()):
+            swap.wait_recv()
         for p in range(PIECES):
-            for way in range(2):
-                if j > hops(way, p):
-                    continue
+            ways = [way for way in range(2) if j <= hops(way, p)]
+            for way in ways:
                 encode(collect(way, j, p, mine(along(way, j), p)), first.at[way, p, j - 1])
+            for way in ways:
                 copy = rs_copy(way, j, p)
                 copy.start()
                 pending.append(copy)
-    done = []
-    for p in range(PIECES):
-        total = mine(z, p)
-        for way in range(2):
-            total = collect(way, 0, p, total)
-        done.append(total)
-    reduced = jnp.transpose(jnp.concatenate(done, axis=0)).astype(BF16)
 
     def place_of(who, d, p):
-        return gath.at[pl.ds(mult(who * half + d // 2 * TILE + p * pr, pr), pr), pl.ds(mult(d % 2 * TILE, TILE), TILE)]
+        return gath.at[pl.ds(mult(p * TILE + d % 2 * pr, pr), pr), pl.ds(mult(who * half + d // 2 * TILE, TILE), TILE)]
 
     def ag_copy(way, j, p, d):
         there = place_of(core, d, p)
@@ -202,58 +199,83 @@
             copy.start()
             pending.append(copy)
 
-    arrivals = []
-
     def share(index, p, d):
         copy = pg_copy(index, p, core, d)
         copy.start()
         pending.append(copy)
-        arrivals.append((index, p, d))
+
+    def receive(j, p):
+        for way in range(2):
+            if j > hops(way, p):
+                continue
+            d = along(1 - way, j)
+            ag_copy(way, j, p, d).wait_recv()
+            spread(way, j, p, d)
+            share(1 + way * nh + j - 1, p, d)
+
+    def receive_shared(p):
+        pg_copy(0, p, 1 - core, z).wait_recv()
+        for j in range(1, nh + 1):
+            for way in range(2):
+                if j <= hops(way, p):
+                    pg_copy(1 + way * nh + j - 1, p, 1 - core, along(1 - way, j)).wait_recv()
 
     for p in range(PIECES):
-        place_of(core, z, p)[...] = reduced[p * pr:(p + 1) * pr]
+        total = mine(z, p)
+        for way in range(2):
+            total = collect(way, 0, p, total)
+        place_of(core, z, p)[...] = total.astype(BF16)
         for way in range(2):
             spread(way, 0, p, z)
-    for p in range(PIECES):
         share(0, p, z)
-    for j in heads[::-1] + near + deep[::-1]:
-        for p in range(PIECES):
-            for way in range(2):
-                if j > hops(way, p):
-                    continue
-                d = along(1 - way, j)
-                ag_copy(way, j, p, d).wait_recv()
-                spread(way, j, p, d)
-                share(1 + way * nh + j - 1, p, d)
-    for index, p, d in arrivals:
-        pg_copy(index, p, 1 - core, d).wait_recv()
-
-    keep = side * side
-    part = dense.shape[0] // keep
+
+    part = dense.shape[0] // (side * side)
     wide = part * side
-    landings = []
+    landings = [[], []]
     order = [side // 2] + [o for o in range(1, side) if o != side // 2] + [0]
-    for ox in order:
+
+    def project(ox, p):
         at = mult((gx + ox) % side * wide, wide)
-        value = jnp.dot(dense[pl.ds(at, wide), :], gath[...], preferred_element_type=F32)
+        value = lax.dot_general(
+            dense[pl.ds(at, wide), :], gath[p * TILE:(p + 1) * TILE, :], (((1,), (1,)), ((), ())),
+            preferred_element_type=F32)
         if ox == 0:
-            yown[...] = value
-        ysend[ox] = value.astype(BF16)
+            yown[p] = value
+        ysend[p, ox] = value.astype(BF16)
         for oy in order:
             if ox == 0 and oy == 0:
                 continue
             index = ox * side + oy
             copy = pltpu.make_async_remote_copy(
-                ysend.at[ox, pl.ds(mult((gy + oy) % side * part, part), part)], yrecv.at[index],
-                y_send.at[index], y_recv.at[index], device_id=peer(ox, oy), device_id_type=MESH)
+                ysend.at[p, ox, pl.ds(mult((gy + oy) % side * part, part), part)], yrecv.at[p, index],
+                y_send.at[p, index], y_recv.at[p, index], device_id=peer(ox, oy), device_id_type=MESH)
             copy.start()
             pending.append(copy)
-            landings.append((index, copy))
-    result = yown[pl.ds(mult(gy * part, part), part), :]
-    for index, copy in landings:
-        copy.wait_recv()
-        result = result + yrecv[index].astype(F32)
-    out_ref[...] = result
+            landings[p].append((index, copy))
+
+    for k in range(len(hints)):
+        pl.semaphore_wait(hint.at[k], 1)
+    for j in heads[::-1]:
+        for p in range(PIECES):
+            receive(j, p)
+    for j in near + deep[::-1]:
+        receive(j, 0)
+    receive_shared(0)
+    later = near + deep[::-1]
+    share_of = -(-len(later) // side)
+    for k, ox in enumerate(order):
+        project(ox, 0)
+        for j in later[k * share_of:(k + 1) * share_of]:
+            receive(j, 1)
+    receive_shared(1)
+    for ox in order:
+        project(ox, 1)
+    for p in range(PIECES):
+        result = yown[p, pl.ds(mult(gy * part, part), part), :]
+        for index, copy in landings[p]:
+            copy.wait_recv()
+            result = result + yrecv[p, index].astype(F32)
+        out_ref[:, p * TILE:(p + 1) * TILE] = result
     for copy in pending:
         copy.wait_send()
 
@@ -292,10 +314,10 @@
                 vmem((nh, rank, TILE), F32),
                 vmem(message, kind),
                 vmem(message, kind),
-                vmem((nz * TILE, rank), BF16),
-                vmem((side, part * side, rank), BF16),
-                vmem((part * side, rank), F32),
-                vmem((side * side, part, rank), BF16),
+                vmem((rank, nz * TILE), BF16),
+                vmem((PIECES, side, part * side, TILE), BF16),
+                vmem((PIECES, part * side, TILE), F32),
+                vmem((PIECES, side * side, part, TILE), BF16),
                 dma((6,)),
                 dma((nh // 2,)),
                 dma((nh // 2,)),
@@ -305,8 +327,9 @@
                 dma((2, PIECES, nh)),
                 dma((1 + 2 * nh, PIECES)),
                 dma((1 + 2 * nh, PIECES)),
-                dma((side * side,)),
-                dma((side * side,)),
+                dma((PIECES, side * side)),
+                dma((PIECES, side * side)),
+                pltpu.SemaphoreType.REGULAR((3,)),
             ],
             compiler_params=pltpu.CompilerParams(
                 collective_id=0, has_side_effects=True, vmem_limit_bytes=67_000_000),

time: 65.7 us -> 63.8 us (0.971)
  Pallas kernels: 63.4 us -> 61.5 us
    pallas_call x1, Pallas kernels: 63.4 us -> 61.5 us  [local(): pl.pallas_call(functools.partial(kernel, nz, side), out_shape=jax.ShapeDt...]
where the time goes in v3:
time: 63.8 us; the launch traced here: 63.7 us
  Pallas kernels  61.5 us (96%)
  local copies, waits for them, and re-layouts  1.47 us (2%)
  between operations  0.66 us (1%)
    pallas_call x1, Pallas kernels, local(): pl.pallas_call(functools.partial(kernel, nz, side), out_shape=jax.ShapeDt...  61.5 us
    unnamed x1, local copies, waits for them, and re-layouts  1.47 us

profile of v3, /device:TPU:1, one launch (start us, length us, event | category | flops | bytes accessed | tf_op | source)
XLA Modules:
  0.0 63.7 jit_solution(12707677789825784197)
XLA Ops:
  0.7 61.5 %power_pass.1 = f32[64,256]{1,0:T(8,128)} custom-call(bf16[1024,256]{1,0:T(8,128)(2,1)} %sketch_hbm.1, bf16[96,128,128]{2,1,0:T(8,128)(2,1)} %tiles_hbm.1, s32[1,96]{1,0:T(1,128)} %bitcast.2, s32[1,96]{1,0:T(1,128)} %bitcast.3, s32[1]{0:T(128)S(6)} %copy.7.count_hbm), custom_call_target="tpu_custom_call" | custom-call | tf_op jit(solution)/shard_map/power_pass/pallas_call | solution.py:297
  62.2 1.5 %copy.8 = f32[64,256]{1,0:T(8,128)} copy(f32[64,256]{1,0:T(8,128)} %power_pass.1) | data formatting | bytes 131072

commit v4 on v3

--- a/solution.py
+++ b/solution.py
@@ -166,18 +166,24 @@
     deep = [j for j in range(nh, 0, -1) if UP[j]]
     heads = [j for j in range(nh, 0, -1) if not UP[j] and children(j, nh)]
     near = [j for j in range(nh, 0, -1) if not UP[j] and not children(j, nh)]
+    def forward(j, p):
+        ways = [way for way in range(2) if j <= hops(way, p)]
+        for way in ways:
+            encode(collect(way, j, p, mine(along(way, j), p)), first.at[way, p, j - 1])
+        for way in ways:
+            copy = rs_copy(way, j, p)
+            copy.start()
+            pending.append(copy)
+
     ready = {deep[0]: swaps[:1], deep[1]: swaps[1:3], deep[-1]: swaps[3:]} if len(swaps) == 4 else {nh: swaps}
-    for j in deep + heads + near:
+    for j in deep or [nh]:
         for swap in ready.get(j, ()):
             swap.wait_recv()
-        for p in range(PIECES):
-            ways = [way for way in range(2) if j <= hops(way, p)]
-            for way in ways:
-                encode(collect(way, j, p, mine(along(way, j), p)), first.at[way, p, j - 1])
-            for way in ways:
-                copy = rs_copy(way, j, p)
-                copy.start()
-                pending.append(copy)
+        if j in deep:
+            forward(j, 0)
+    for p, group in ((1, deep), (0, heads + near), (1, heads + near)):
+        for j in group:
+            forward(j, p)
 
     def place_of(who, d, p):
         return gath.at[pl.ds(mult(p * TILE + d % 2 * pr, pr), pr), pl.ds(mult(who * half + d // 2 * TILE, TILE), TILE)]
@@ -255,29 +261,32 @@
 
     for k in range(len(hints)):
         pl.semaphore_wait(hint.at[k], 1)
-    for j in heads[::-1]:
-        for p in range(PIECES):
+    for p in range(PIECES):
+        for j in heads[::-1]:
             receive(j, p)
     for j in near + deep[::-1]:
         receive(j, 0)
     receive_shared(0)
     later = near + deep[::-1]
-    share_of = -(-len(later) // side)
+    taken = (0, 0, 3, 4)
     for k, ox in enumerate(order):
         project(ox, 0)
-        for j in later[k * share_of:(k + 1) * share_of]:
+        for j in later[taken[k]:taken[k + 1] if k + 1 < side else len(later)]:
             receive(j, 1)
     receive_shared(1)
     for ox in order:
         project(ox, 1)
-    for p in range(PIECES):
+    def finish(p):
         result = yown[p, pl.ds(mult(gy * part, part), part), :]
         for index, copy in landings[p]:
             copy.wait_recv()
             result = result + yrecv[p, index].astype(F32)
         out_ref[:, p * TILE:(p + 1) * TILE] = result
+
+    finish(0)
     for copy in pending:
         copy.wait_send()
+    finish(1)
 
 
 def solution(mesh):

time: 63.8 us -> 61 us (0.956)
  Pallas kernels: 61.5 us -> 58.7 us
    pallas_call x1, Pallas kernels: 61.5 us -> 58.7 us  [local(): pl.pallas_call(functools.partial(kernel, nz, side), out_shape=jax.ShapeDt...]
where the time goes in v4:
time: 61 us; the launch traced here: 60.8 us
  Pallas kernels  58.7 us (96%)
  local copies, waits for them, and re-layouts  1.47 us (2%)
  between operations  0.66 us (1%)
    pallas_call x1, Pallas kernels, local(): pl.pallas_call(functools.partial(kernel, nz, side), out_shape=jax.ShapeDt...  58.7 us
    unnamed x1, local copies, waits for them, and re-layouts  1.47 us

profile of v4, /device:TPU:1, one launch (start us, length us, event | category | flops | bytes accessed | tf_op | source)
XLA Modules:
  0.0 60.8 jit_solution(14080436554309097744)
XLA Ops:
  0.7 58.7 %power_pass.1 = f32[64,256]{1,0:T(8,128)} custom-call(bf16[1024,256]{1,0:T(8,128)(2,1)} %sketch_hbm.1, bf16[96,128,128]{2,1,0:T(8,128)(2,1)} %tiles_hbm.1, s32[1,96]{1,0:T(1,128)} %bitcast.2, s32[1,96]{1,0:T(1,128)} %bitcast.3, s32[1]{0:T(128)S(6)} %copy.7.count_hbm), custom_call_target="tpu_custom_call" | custom-call | tf_op jit(solution)/shard_map/power_pass/pallas_call | solution.py:306
  59.4 1.5 %copy.8 = f32[64,256]{1,0:T(8,128)} copy(f32[64,256]{1,0:T(8,128)} %power_pass.1) | data formatting | bytes 131072

commit v5 on v4

--- a/solution.py
+++ b/solution.py
@@ -12,7 +12,7 @@
 PIECES = 2
 CODED = True
 PEAK = 32700.0
-SCALE_ROWS = 16
+SCALE_ROWS = 8
 ORDER = (2, 1, 3, 0)
 UP = {1: 0, 2: 0, 3: 2, 4: 2, 5: 0, 6: 5, 7: 5, 8: 5}
 F32 = jnp.float32

time: 61 us -> 58.8 us (0.964)
  Pallas kernels: 58.7 us -> 56.5 us
    pallas_call x1, Pallas kernels: 58.7 us -> 56.5 us  [local(): pl.pallas_call(functools.partial(kernel, nz, side), out_shape=jax.ShapeDt...]
where the time goes in v5:
time: 58.8 us; the launch traced here: 58.7 us
  Pallas kernels  56.5 us (96%)
  local copies, waits for them, and re-layouts  1.47 us (2%)
  between operations  0.66 us (1%)
    pallas_call x1, Pallas kernels, local(): pl.pallas_call(functools.partial(kernel, nz, side), out_shape=jax.ShapeDt...  56.5 us
    unnamed x1, local copies, waits for them, and re-layouts  1.47 us

profile of v5, /device:TPU:1, one launch (start us, length us, event | category | flops | bytes accessed | tf_op | source)
XLA Modules:
  0.0 58.7 jit_solution(18400656429656820481)
XLA Ops:
  0.7 56.5 %power_pass.1 = f32[64,256]{1,0:T(8,128)} custom-call(bf16[1024,256]{1,0:T(8,128)(2,1)} %sketch_hbm.1, bf16[96,128,128]{2,1,0:T(8,128)(2,1)} %tiles_hbm.1, s32[1,96]{1,0:T(1,128)} %bitcast.2, s32[1,96]{1,0:T(1,128)} %bitcast.3, s32[1]{0:T(128)S(6)} %copy.7.count_hbm), custom_call_target="tpu_custom_call" | custom-call | tf_op jit(solution)/shard_map/power_pass/pallas_call | solution.py:306
  57.2 1.5 %copy.8 = f32[64,256]{1,0:T(8,128)} copy(f32[64,256]{1,0:T(8,128)} %power_pass.1) | data formatting | bytes 131072
